TPU v7x, 32 devices: a whole 2x2x4 slice. The times are simulated.
32 devices in a mesh: grp: 4 (over y, x), blk: 8 (over z, core).
Axes of the slice: x: 2, y: 2, z: 4, core: 2. Of those that a mesh axis runs over, the one named last changes fastest.
Arguments:
- student: bfloat16 [6144, 1024], P(('grp', 'blk')), parts along dimension 0, may hold values from -6 to 6
- teacher: bfloat16 [6144, 1024], P(('grp', 'blk')), parts along dimension 0, may hold values from -6 to 6
Outputs:
- grad_student: float32 [6144, 1024], P(('grp', 'blk')), parts along dimension 0
There are 4 independent parts, one for each index of `grp`. A program takes and returns all parts, laid end to end along the dimension named above; each array names one. Nothing has to cross between parts.
All inputs are finite; a program needn't handle non-finite values.
Results may differ from a plain program's by a relative error of at most 0.01.
Values may be sent and summed in bfloat16 or wider, within the bound.
No kernel may reach another device: no remote copies, remote signals or barrier semaphores. Data moves between devices by JAX's collectives and lax.ppermute only.
A program may use at most 128 MiB of HBM per device.

v0:
```python
import jax
import jax.numpy as jnp
from jax import lax
from jax.sharding import PartitionSpec as P

D = 1024


def normalize(values):
    floats = values.astype(jnp.float32)
    norms = jnp.sqrt(jnp.sum(floats * floats, axis=1, keepdims=True) + 1e-06)
    return (floats / norms, norms)


def split_product(left, right):
    left_hi = left.astype(jnp.bfloat16)
    left_lo = (left - left_hi.astype(jnp.float32)).astype(jnp.bfloat16)
    return jnp.dot(left_hi, right, preferred_element_type=jnp.float32) + jnp.dot(
        left_lo, right, preferred_element_type=jnp.float32
    )


def body(student, teacher):
    row_count = student.shape[0]
    text_count = row_count * lax.axis_size("blk")
    s_float, norm_h = normalize(student)
    s_half = s_float.astype(jnp.bfloat16)
    t_float, teacher_norm = normalize(teacher)
    t_half = t_float.astype(jnp.bfloat16)
    s_wide = s_half.astype(jnp.float32)
    s_piece = lax.all_gather(s_half, "blk", axis=0, tiled=True)
    t_piece = lax.all_gather(t_half, "blk", axis=0, tiled=True)
    gram_s = lax.dot_general(
        s_half, s_piece, (((1,), (1,)), ((), ())), preferred_element_type=jnp.float32
    )
    gram_t = lax.dot_general(
        t_half, t_piece, (((1,), (1,)), ((), ())), preferred_element_type=jnp.float32
    )
    product = split_product(gram_s - gram_t, s_piece)
    g_s = product * (D / jnp.sqrt(jnp.float32(text_count)))
    along = jnp.sum(s_wide * g_s, axis=1, keepdims=True)
    return (g_s - s_wide * along) / norm_h


def solution(mesh):
    in_specs = (P(("grp", "blk"), None), P(("grp", "blk"), None))
    out_specs = P(("grp", "blk"), None)
    return jax.shard_map(body, mesh=mesh, in_specs=in_specs, out_specs=out_specs, check_vma=False)
```

profile of v0, /device:TPU:0, one launch (start us, length us, event | category | flops | bytes accessed | tf_op | source)
XLA Modules:
  0.0 102.9 jit_solution(4346751903632216425)
XLA Ops:
  6.5 0.0 all-gather.3.cloned.1.call-start
  6.5 1.2 %fusion.1 = f32[192]{0:T(256)S(1)} fusion(bf16[192,1024]{1,0:T(8,128)(2,1)} %param.2), kind=kLoop, calls=%fused_computation.10 | loop fusion | flops 589632 | bytes 393984 | tf_op jit(solution)/shard_map/reduce_sum | solution.py:11
  7.7 1.9 %fusion.2 = bf16[192,1024]{1,0:T(8,128)(2,1)} fusion(bf16[192,1024]{1,0:T(8,128)(2,1)} %param.2, f32[192]{0:T(256)S(1)} %add_sqrt_fusion.1), kind=kLoop, calls=%fused_computation.11 | loop fusion | flops 589824 | bytes 787200 | tf_op jit(solution)/shard_map/convert_element_type | solution.py:27
  9.6 0.0 all-gather.3.cloned.1.call-update
  9.6 0.0 all-gather.5.cloned.1.call-start
  9.7 1.2 %fusion.3 = f32[192]{0:T(256)S(1)} fusion(bf16[192,1024]{1,0:T(8,128)(2,1)} %param.3), kind=kLoop, calls=%fused_computation.12 | loop fusion | flops 589632 | bytes 393984 | tf_op jit(solution)/shard_map/reduce_sum | solution.py:11
  10.8 1.9 %fusion.4 = bf16[192,1024]{1,0:T(8,128)(2,1)} fusion(bf16[192,1024]{1,0:T(8,128)(2,1)} %param.3, f32[192]{0:T(256)S(1)} %add_sqrt_fusion), kind=kLoop, calls=%fused_computation.13 | loop fusion | flops 589824 | bytes 787200 | tf_op jit(solution)/shard_map/convert_element_type | solution.py:29
  12.7 0.0 copy-start.2
  12.7 0.0 all-gather.5.cloned.1.call-update
  12.8 38.0 %all-gather.3.cloned.1.call-done = bf16[1536,1024]{1,0:T(8,128)(2,1)} async-done(((bf16[192,1024]{1,0:T(8,128)(2,1)}), bf16[1536,1024]{1,0:T(8,128)(2,1)}) %all-gather.3.cloned.1.call-update) | async-done | bytes 3145744 | tf_op jit(solution)/shard_map/all_gather | solution.py:31
  50.7 4.2 %fusion.11 = f32[192,1536]{1,0:T(8,128)} fusion(bf16[192,1024]{1,0:T(8,128)(2,1)} %fusion.2, bf16[1536,1024]{1,0:T(8,128)(2,1)} %all-gather.3.cloned.1.call-done), kind=kOutput, calls=%fused_computation.22 | convolution fusion | flops 603979776 | bytes 4718592 | tf_op jit(solution)/shard_map/dot_general | solution.py:33
  55.0 0.0 copy-start
  55.0 34.5 %all-gather.5.cloned.1.call-done = bf16[1536,1024]{1,0:T(8,128)(2,1)} async-done(((bf16[192,1024]{1,0:T(8,128)(2,1)}), bf16[1536,1024]{1,0:T(8,128)(2,1)}) %all-gather.5.cloned.1.call-update) | async-done | bytes 3145744 | tf_op jit(solution)/shard_map/all_gather | solution.py:32
  89.5 0.0 copy-done.2
  89.5 3.4 %convolution_subtract_fusion = f32[192,1536]{1,0:T(8,128)S(1)} fusion(f32[192,1536]{1,0:T(8,128)} %fusion.11, bf16[192,1024]{1,0:T(8,128)(2,1)S(1)} %copy-done.2, bf16[1536,1024]{1,0:T(8,128)(2,1)} %all-gather.5.cloned.1.call-done), kind=kOutput, calls=%fused_computation | convolution fusion | flops 604274688 | bytes 5898240 | tf_op jit(solution)/shard_map/dot_general | solution.py:36
  92.9 0.0 copy-done
  92.9 0.0 copy-start.1
  93.0 0.8 fusion.9
  93.8 0.2 copy-done.1
  93.9 0.0 copy-start.3
  93.9 1.0 fusion.5
  94.9 0.0 copy-done.3
  94.9 1.1 %fusion.7 = f32[192,1024]{1,0:T(8,128)} fusion(f32[192,1024]{1,0:T(8,128)S(1)} %get-tuple-element.6, f32[192]{0:T(256)S(1)} %get-tuple-element.5, f32[192]{0:T(256)S(1)} %add_sqrt_fusion.1, bf16[192,1024]{1,0:T(8,128)(2,1)S(1)} %copy-done.3), kind=kLoop, calls=%fused_computation.16 | loop fusion | flops 1376256 | bytes 1967616 | tf_op jit(solution)/shard_map/div | solution.py:42
  (2 shorter events, 0.0 us)
Async XLA Ops:
  6.5 44.2 %all-gather.3.cloned.1.call-start = ((), (), s32[]{:S(2)}) async-start(), calls=%async_computation | async-start | bytes 3538944 | tf_op jit(solution)/shard_map/all_gather | solution.py:31
  9.6 79.9 %all-gather.5.cloned.1.call-start = ((), (), s32[]{:S(2)}) async-start(), calls=%async_computation.1 | async-start | bytes 3538944 | tf_op jit(solution)/shard_map/all_gather | solution.py:32
  12.7 76.8 %copy-start.2 = (bf16[192,1024]{1,0:T(8,128)(2,1)S(1)}, bf16[192,1024]{1,0:T(8,128)(2,1)}, u32[]{:S(2)}) copy-start(bf16[192,1024]{1,0:T(8,128)(2,1)} %fusion.4) | copy-start | bytes 1179652
  55.0 38.0 %copy-start = (bf16[1536,1024]{1,0:T(8,128)(2,1)S(1)}, bf16[1536,1024]{1,0:T(8,128)(2,1)}, u32[]{:S(2)}) copy-start(bf16[1536,1024]{1,0:T(8,128)(2,1)} %all-gather.3.cloned.1.call-done) | copy-start | bytes 9437188
  92.9 1.0 copy-start.1
  93.9 1.0 copy-start.3
Sparse Core Ops, SparseCore 0:
  9.7 40.9 all-gather.2
  52.4 37.1 all-gather.4
where the time goes:
time: 103 us
  waiting for transfers between devices  72.5 us (70%)
  between operations  13.4 us (13%)
  matrix products  9.43 us (9%)
  other arithmetic  7.21 us (7%)
    all_gather x1, waiting for transfers between devices, body(): s_piece = lax.all_gather(s_half, 'blk', axis=0, tiled=True)  38 us
    all_gather x1, waiting for transfers between devices, body(): t_piece = lax.all_gather(t_half, 'blk', axis=0, tiled=True)  34.5 us
    dot_general x1, matrix products, body(): lax.dot_general(s_half, s_piece, (((1,), (1,)), ((), ())), preferred_elem...  4.25 us
    dot_general x1, matrix products, body(): lax.dot_general(t_half, t_piece, (((1,), (1,)), ((), ())), preferred_elem...  3.4 us
    reduce_sum x2, other arithmetic, normalize(): norms = jnp.sqrt(jnp.sum(floats * floats, axis=1, keepdims=True) + 1e-06)  2.31 us
  transfers between devices with their start and end apart: 2, of which 2 were waited for; matrix products, arithmetic and copies ran while one was open for 7% of the time, Pallas kernels for 0%

commit v1 on v0

--- a/solution.py
+++ b/solution.py
@@ -28,7 +28,13 @@
     t_float, teacher_norm = normalize(teacher)
     t_half = t_float.astype(jnp.bfloat16)
     s_wide = s_half.astype(jnp.float32)
-    s_piece = lax.all_gather(s_half, "blk", axis=0, tiled=True)
+    devices = lax.axis_size("blk")
+    current, parts = (s_half, [s_half])
+    for _ in range(devices - 1):
+        current = lax.ppermute(current, "blk", [(i, (i + 1) % devices) for i in range(devices)])
+        parts.insert(0, current)
+    line = jnp.concatenate(parts, axis=0)
+    s_piece = jnp.roll(line, (lax.axis_index("blk") + 1) * s_half.shape[0], axis=0)
     t_piece = lax.all_gather(t_half, "blk", axis=0, tiled=True)
     gram_s = lax.dot_general(
         s_half, s_piece, (((1,), (1,)), ((), ())), preferred_element_type=jnp.float32

time: 103 us -> 129 us (1.25)
  local copies, waits for them, and re-layouts: 0.2 us -> 13 us
  waiting for transfers between devices: 72.5 us -> 80.7 us
  matrix products: 9.43 us -> 12.2 us
    ppermute x0 -> x7, waiting for transfers between devices: none -> 80.7 us  [body(): lax.ppermute(current, 'blk', [(i, (i + 1) % devices) for i in range(devic...]
    all_gather x1 -> x0, waiting for transfers between devices: 38 us -> none  [body(): s_piece = lax.all_gather(s_half, 'blk', axis=0, tiled=True)]
    all_gather x1, waiting for transfers between devices: 34.5 us -> 0.01 us  [body(): t_piece = lax.all_gather(t_half, 'blk', axis=0, tiled=True)]
    unnamed x8 -> x18, local copies, waits for them, and re-layouts: 0.2 us -> 13 us
    dot_general x1, matrix products: 0.8 us -> 3.1 us  [split_product(): jnp.dot(left_hi, right, preferred_element_type=jnp.float32)]
    dot_general x1, matrix products: 0.98 us -> 2.92 us  [split_product(): jnp.dot(left_lo, right, preferred_element_type=jnp.float32)]
  transfers between devices with their start and end apart: 2 -> 8, of which waited for: 2 -> 7; matrix products, arithmetic and copies ran while one was open for 7% -> 13% of each run, Pallas kernels for 0% -> 0%
where the time goes in v1:
time: 129 us; the launch traced here: 128 us
  waiting for transfers between devices  80.7 us (63%)
  between operations  13.4 us (10%)
  local copies, waits for them, and re-layouts  13 us (10%)
  matrix products  12.2 us (9%)
  other arithmetic  8.35 us (6%)
    ppermute x7, waiting for transfers between devices, body(): lax.ppermute(current, 'blk', [(i, (i + 1) % devices) for i in range(devic...  80.7 us
    unnamed x18, local copies, waits for them, and re-layouts  13 us
    dot_general x1, matrix products, body(): lax.dot_general(s_half, s_piece, (((1,), (1,)), ((), ())), preferred_elem...  3.11 us
    dot_general x1, matrix products, split_product(): jnp.dot(left_hi, right, preferred_element_type=jnp.float32)  3.1 us
    dot_general x1, matrix products, body(): lax.dot_general(t_half, t_piece, (((1,), (1,)), ((), ())), preferred_elem...  3.07 us
    dot_general x1, matrix products, split_product(): jnp.dot(left_lo, right, preferred_element_type=jnp.float32)  2.92 us
  transfers between devices with their start and end apart: 8, of which 7 were waited for; matrix products, arithmetic and copies ran while one was open for 13% of the time, Pallas kernels for 0%

profile of v1, /device:TPU:0, one launch (start us, length us, event | category | flops | bytes accessed | tf_op | source)
XLA Modules:
  0.0 128.2 jit_solution(355845835469750470)
XLA Ops:
  6.5 0.0 copy-start
  6.5 0.0 all-gather.2.cloned.1.call-start
  6.5 1.2 fusion.13
  7.8 1.9 %fusion.14 = bf16[192,1024]{1,0:T(8,128)(2,1)} fusion(bf16[192,1024]{1,0:T(8,128)(2,1)} %param.3, f32[192]{0:T(256)S(1)} %add_sqrt_fusion), kind=kLoop, calls=%fused_computation.18 | loop fusion | flops 589824 | bytes 787200 | tf_op jit(solution)/shard_map/convert_element_type | solution.py:29
  9.7 0.0 all-gather.2.cloned.1.call-update
  9.7 1.2 fusion.11
  10.8 1.2 fusion.12
  12.0 0.5 collective-permute-start
  12.5 9.5 %collective-permute-done = bf16[192,1024]{1,0:T(8,128)(2,1)S(1)} collective-permute-done((bf16[192,1024]{1,0:T(8,128)(2,1)S(1)}, bf16[192,1024]{1,0:T(8,128)(2,1)S(1)}, u32[]{:S(2)}, u32[]{:S(2)}) %collective-permute-start) | collective-permute-done | bytes 393248 | tf_op jit(solution)/shard_map/ppermute | solution.py:34
  22.0 0.0 collective-permute-start.1
  22.0 17.6 %collective-permute-done.1 = bf16[192,1024]{1,0:T(8,128)(2,1)S(1)} collective-permute-done((bf16[192,1024]{1,0:T(8,128)(2,1)S(1)}, bf16[192,1024]{1,0:T(8,128)(2,1)S(1)}, u32[]{:S(2)}, u32[]{:S(2)}) %collective-permute-start.1) | collective-permute-done | bytes 393248 | tf_op jit(solution)/shard_map/ppermute | solution.py:34
  39.6 0.0 collective-permute-start.2
  39.6 17.5 %collective-permute-done.2 = bf16[192,1024]{1,0:T(8,128)(2,1)S(1)} collective-permute-done((bf16[192,1024]{1,0:T(8,128)(2,1)S(1)}, bf16[192,1024]{1,0:T(8,128)(2,1)S(1)}, u32[]{:S(2)}, u32[]{:S(2)}) %collective-permute-start.2) | collective-permute-done | bytes 393248 | tf_op jit(solution)/shard_map/ppermute | solution.py:34
  57.1 0.0 collective-permute-start.3
  57.1 9.0 %collective-permute-done.3 = bf16[192,1024]{1,0:T(8,128)(2,1)S(1)} collective-permute-done((bf16[192,1024]{1,0:T(8,128)(2,1)S(1)}, bf16[192,1024]{1,0:T(8,128)(2,1)S(1)}, u32[]{:S(2)}, u32[]{:S(2)}) %collective-permute-start.3) | collective-permute-done | bytes 393248 | tf_op jit(solution)/shard_map/ppermute | solution.py:34
  66.1 0.0 collective-permute-start.4
  66.1 9.0 %collective-permute-done.4 = bf16[192,1024]{1,0:T(8,128)(2,1)S(1)} collective-permute-done((bf16[192,1024]{1,0:T(8,128)(2,1)S(1)}, bf16[192,1024]{1,0:T(8,128)(2,1)S(1)}, u32[]{:S(2)}, u32[]{:S(2)}) %collective-permute-start.4) | collective-permute-done | bytes 393248 | tf_op jit(solution)/shard_map/ppermute | solution.py:34
  75.1 0.0 collective-permute-start.5
  75.1 9.0 %collective-permute-done.5 = bf16[192,1024]{1,0:T(8,128)(2,1)S(1)} collective-permute-done((bf16[192,1024]{1,0:T(8,128)(2,1)S(1)}, bf16[192,1024]{1,0:T(8,128)(2,1)S(1)}, u32[]{:S(2)}, u32[]{:S(2)}) %collective-permute-start.5) | collective-permute-done | bytes 393248 | tf_op jit(solution)/shard_map/ppermute | solution.py:34
  84.1 0.0 collective-permute-start.6
  84.1 0.0 copy-start.1
  84.1 9.1 %collective-permute-done.6 = bf16[192,1024]{1,0:T(8,128)(2,1)} collective-permute-done((bf16[192,1024]{1,0:T(8,128)(2,1)S(1)}, bf16[192,1024]{1,0:T(8,128)(2,1)}, u32[]{:S(2)}, u32[]{:S(2)}) %collective-permute-start.6) | collective-permute-done | bytes 393248 | tf_op jit(solution)/shard_map/ppermute | solution.py:34
  93.2 1.8 %constant_dynamic-update-slice_fusion.15 = bf16[3072,1024]{1,0:T(8,128)(2,1)} fusion(bf16[192,1024]{1,0:T(8,128)(2,1)} %collective-permute-done.6), kind=kLoop, calls=%fused_computation.39 | loop fusion | bytes 786432
  95.0 0.8 constant_dynamic-update-slice_fusion.14
  95.8 0.8 constant_dynamic-update-slice_fusion.13
  96.6 0.8 constant_dynamic-update-slice_fusion.12
  97.4 0.8 constant_dynamic-update-slice_fusion.11
  98.1 0.8 constant_dynamic-update-slice_fusion.10
  99.0 0.8 constant_dynamic-update-slice_fusion.9
  99.7 0.0 copy-done
  99.7 0.9 constant_dynamic-update-slice_fusion.8
  100.7 1.8 %constant_dynamic-update-slice_fusion.7 = bf16[3072,1024]{1,0:T(8,128)(2,1)} fusion(bf16[3072,1024]{1,0:T(8,128)(2,1)} %constant_dynamic-update-slice_fusion.8, bf16[192,1024]{1,0:T(8,128)(2,1)} %collective-permute-done.6), kind=kLoop, calls=%fused_computation.31 | loop fusion | bytes 786432
  102.4 0.8 constant_dynamic-update-slice_fusion.6
  103.2 0.8 constant_dynamic-update-slice_fusion.5
  104.0 0.8 constant_dynamic-update-slice_fusion.4
  104.8 0.8 constant_dynamic-update-slice_fusion.3
  105.6 0.8 constant_dynamic-update-slice_fusion.2
  106.3 0.8 constant_dynamic-update-slice_fusion.1
  107.2 0.9 constant_dynamic-update-slice_fusion
  108.1 0.0 all-gather.2.cloned.1.call-done
  108.1 0.0 copy-done.1
  108.1 3.1 %fusion.23 = f32[192,1536]{1,0:T(8,128)S(1)} fusion(bf16[192,1024]{1,0:T(8,128)(2,1)S(1)} %copy-done.1, bf16[1536,1024]{1,0:T(8,128)(2,1)} %all-gather.2.cloned.1.call-done), kind=kOutput, calls=%fused_computation.45 | convolution fusion | flops 603979776 | bytes 4718592 | tf_op jit(solution)/shard_map/dot_general | solution.py:42
  111.1 3.1 %convolution_subtract_fusion = f32[192,1536]{1,0:T(8,128)S(1)} fusion(f32[192,1536]{1,0:T(8,128)S(1)} %fusion.23, bf16[192,1024]{1,0:T(8,128)(2,1)S(1)} %fusion.12, bf16[3072,1024]{1,0:T(8,128)(2,1)} %constant_dynamic-update-slice_fusion, s32[]{:T(128)S(6)} %select_n.14), kind=kOutput, calls=%fused_computation | convolution fusion | flops 604274688 | bytes 5898244 | tf_op jit(solution)/shard_map/dot_general | solution.py:39
  114.2 2.9 %fusion = f32[192,1024]{1,0:T(8,128)S(1)} fusion(bf16[3072,1024]{1,0:T(8,128)(2,1)} %constant_dynamic-update-slice_fusion, s32[]{:T(128)S(6)} %select_n.14, f32[192,1536]{1,0:T(8,128)S(1)} %convolution_subtract_fusion), kind=kOutput, calls=%fused_computation.1 | convolution fusion | flops 605159424 | bytes 5111812 | tf_op jit(solution)/shard_map/dot_general | solution.py:18
  117.2 3.1 %fusion.15 = (f32[192]{0:T(256)S(1)}, f32[192,1024]{1,0:T(8,128)S(1)}) fusion(bf16[192,1024]{1,0:T(8,128)(2,1)S(1)} %fusion.12, f32[192,1024]{1,0:T(8,128)S(1)} %fusion, bf16[3072,1024]{1,0:T(8,128)(2,1)} %constant_dynamic-update-slice_fusion, s32[]{:T(128)S(6)} %select_n.14, f32[192,1536]{1,0:T(8,128)S(1)} %convolution_subtract_fusion), kind=kOutput, calls=%fused_computation.19 | convolution fusion | flops 605257536 | bytes 6292228 | tf_op jit(solution)/shard_map/dot_general | solution.py:18
  120.3 1.1 fusion.17
  (2 shorter events, 0.0 us)
Async XLA Ops:
  6.5 93.2 %copy-start = (bf16[192,1024]{1,0:T(8,128)(2,1)S(1)}, bf16[192,1024]{1,0:T(8,128)(2,1)}, u32[]{:S(2)}) copy-start(bf16[192,1024]{1,0:T(8,128)(2,1)} %param.2) | copy-start | bytes 1179652
  6.5 101.5 %all-gather.2.cloned.1.call-start = ((), (), s32[]{:S(2)}) async-start(), calls=%async_computation | async-start | bytes 3538944 | tf_op jit(solution)/shard_map/all_gather | solution.py:38
  12.0 10.0 %collective-permute-start = (bf16[192,1024]{1,0:T(8,128)(2,1)S(1)}, bf16[192,1024]{1,0:T(8,128)(2,1)S(1)}, u32[]{:S(2)}, u32[]{:S(2)}) collective-permute-start(bf16[192,1024]{1,0:T(8,128)(2,1)S(1)} %fusion.12), channel_id=1, source_target_pairs={{0,1},{1,2},{2,3},{3,4},{4,5},{5,6},{6,7},{7,0},{8,9},{9,10},{10,1... | collective-permute-start | bytes 1179656 | tf_op jit(solution)/shard_map/ppermute | solution.py:34
  22.0 17.6 %collective-permute-start.1 = (bf16[192,1024]{1,0:T(8,128)(2,1)S(1)}, bf16[192,1024]{1,0:T(8,128)(2,1)S(1)}, u32[]{:S(2)}, u32[]{:S(2)}) collective-permute-start(bf16[192,1024]{1,0:T(8,128)(2,1)S(1)} %collective-permute-done), channel_id=1, source_target_pairs={{0,1},{1,2},{2,3},{3,4},{4,5},{5,6},{6,7},{7,0},{8,9},{9,10},{10,1... | collective-permute-start | bytes 1179656 | tf_op jit(solution)/shard_map/ppermute | solution.py:34
  39.6 17.6 %collective-permute-start.2 = (bf16[192,1024]{1,0:T(8,128)(2,1)S(1)}, bf16[192,1024]{1,0:T(8,128)(2,1)S(1)}, u32[]{:S(2)}, u32[]{:S(2)}) collective-permute-start(bf16[192,1024]{1,0:T(8,128)(2,1)S(1)} %collective-permute-done.1), channel_id=1, source_target_pairs={{0,1},{1,2},{2,3},{3,4},{4,5},{5,6},{6,7},{7,0},{8,9},{9,10},{10,1... | collective-permute-start | bytes 1179656 | tf_op jit(solution)/shard_map/ppermute | solution.py:34
  57.1 9.0 %collective-permute-start.3 = (bf16[192,1024]{1,0:T(8,128)(2,1)S(1)}, bf16[192,1024]{1,0:T(8,128)(2,1)S(1)}, u32[]{:S(2)}, u32[]{:S(2)}) collective-permute-start(bf16[192,1024]{1,0:T(8,128)(2,1)S(1)} %collective-permute-done.2), channel_id=1, source_target_pairs={{0,1},{1,2},{2,3},{3,4},{4,5},{5,6},{6,7},{7,0},{8,9},{9,10},{10,1... | collective-permute-start | bytes 1179656 | tf_op jit(solution)/shard_map/ppermute | solution.py:34
  66.1 9.0 %collective-permute-start.4 = (bf16[192,1024]{1,0:T(8,128)(2,1)S(1)}, bf16[192,1024]{1,0:T(8,128)(2,1)S(1)}, u32[]{:S(2)}, u32[]{:S(2)}) collective-permute-start(bf16[192,1024]{1,0:T(8,128)(2,1)S(1)} %collective-permute-done.3), channel_id=1, source_target_pairs={{0,1},{1,2},{2,3},{3,4},{4,5},{5,6},{6,7},{7,0},{8,9},{9,10},{10,1... | collective-permute-start | bytes 1179656 | tf_op jit(solution)/shard_map/ppermute | solution.py:34
  75.1 9.0 %collective-permute-start.5 = (bf16[192,1024]{1,0:T(8,128)(2,1)S(1)}, bf16[192,1024]{1,0:T(8,128)(2,1)S(1)}, u32[]{:S(2)}, u32[]{:S(2)}) collective-permute-start(bf16[192,1024]{1,0:T(8,128)(2,1)S(1)} %collective-permute-done.4), channel_id=1, source_target_pairs={{0,1},{1,2},{2,3},{3,4},{4,5},{5,6},{6,7},{7,0},{8,9},{9,10},{10,1... | collective-permute-start | bytes 1179656 | tf_op jit(solution)/shard_map/ppermute | solution.py:34
  84.1 9.1 %collective-permute-start.6 = (bf16[192,1024]{1,0:T(8,128)(2,1)S(1)}, bf16[192,1024]{1,0:T(8,128)(2,1)}, u32[]{:S(2)}, u32[]{:S(2)}) collective-permute-start(bf16[192,1024]{1,0:T(8,128)(2,1)S(1)} %collective-permute-done.5), channel_id=1, source_target_pairs={{0,1},{1,2},{2,3},{3,4},{4,5},{5,6},{6,7},{7,0},{8,9},{9,10},{10,1... | collective-permute-start | bytes 1179656 | tf_op jit(solution)/shard_map/ppermute | solution.py:34
  84.1 23.9 %copy-start.1 = (bf16[192,1024]{1,0:T(8,128)(2,1)S(1)}, bf16[192,1024]{1,0:T(8,128)(2,1)}, u32[]{:S(2)}) copy-start(bf16[192,1024]{1,0:T(8,128)(2,1)} %fusion.14) | copy-start | bytes 1179652
Sparse Core Ops, SparseCore 0:
  9.8 49.3 all-gather.1
